TPU v7x, 32 devices: a whole 2x2x4 slice. The times are simulated.
32 devices in a mesh: rows: 8 (over z, y), vecs: 4 (over x, core).
Axes of the slice: x: 2, y: 2, z: 4, core: 2. Of those that a mesh axis runs over, the one named last changes fastest.
Arguments:
- vectors: bfloat16 [24576, 512], P('rows', 'vecs'), may hold values from -8 to 8
- node_mass: float32 [24576], P('rows'), may hold values from 0.5 to 2
- cable_stiff: float32 [24576], P('rows'), may hold values from 0.1 to 1
- cable_nodes: int32 [8, 4], P('rows'), may hold values from 1 to 1152, 2304 in all within a row
- deck_rigidity: float32 [], replicated, may hold values from 0.3 to 1
- anchor_rows: int32 [8, 8, 4], P('rows'), may hold values from 0 to 3072, as said below
- anchor_stiff: float32 [8, 8, 4], P('rows'), may hold values from 0.2 to 1, as said below
- cut_low: float32 [], replicated, may hold values from 1.5 to 2.5
- top_bound: float32 [], replicated, may hold values from 7 to 9
Outputs:
- basis: bfloat16 [24576, 512], P('rows', 'vecs')
Inputs may be any that keep to these rules, and one draw needn't show every extreme that they name: anchor_rows[r, q, s] is a node of partition r coupled through slot s to partition q, or 3072 where the slot is empty; slot s of r towards q is live exactly when slot s of q towards r is; live slots come first; no partition has live slots towards itself; a partition that is not a pylon partition has live slots only towards the partitions beside it in the cyclic order, which fill all 4 slots, and towards at most 4 pylon partitions; pylon partitions come in pairs half the cyclic order apart, and the two of a pair fill all 4 slots towards each other. anchor_stiff[r, q, s] equals anchor_stiff[q, r, s].
All inputs are finite; a program needn't handle non-finite values.
Results may differ from a plain program's by a relative error of at most 0.0072.
The roundings to bfloat16 on the way count: a program that leaves them out, or rounds other values in their place, can miss the bound.
Values may be sent and summed in bfloat16 or wider, within the bound.
A program may use at most 64 MiB of HBM per device.

v0:
```python
import jax
import jax.numpy as jnp
from jax import lax
from jax.sharding import PartitionSpec as P

CABLE_ROWS = 2304


def with_halo(block, sides, width):
    for axis, dim in sides:
        count = lax.axis_size(axis)
        forward = [(i, i + 1) for i in range(count - 1)]
        backward = [(target, source) for source, target in forward]
        low = lax.ppermute(
            lax.slice_in_dim(block, block.shape[dim] - width, None, axis=dim), axis, forward
        )
        high = lax.ppermute(lax.slice_in_dim(block, 0, width, axis=dim), axis, backward)
        block = jnp.concatenate([low, block, high], axis=dim)
    return block


def body(
    vectors,
    node_mass,
    cable_stiff,
    cable_nodes,
    deck_rigidity,
    anchor_rows,
    anchor_stiff,
    cut_low,
    top_bound,
):
    part_count = lax.axis_size("rows")
    my_index = lax.axis_index("rows")
    own_width = vectors.shape[1]
    cable_ends = jnp.cumsum(cable_nodes[0])
    positions = jnp.arange(CABLE_ROWS - 1, dtype=jnp.int32) + 1
    breaks = jnp.any(positions[:, None] == cable_ends[None, :], axis=1)
    cable_links = jnp.where(breaks, 0.0, cable_stiff[: CABLE_ROWS - 1])[:, None]
    left_open = jnp.where(my_index > 0, deck_rigidity, 0.0)
    right_open = jnp.where(my_index < part_count - 1, deck_rigidity, 0.0)
    slot_rows = anchor_rows[0]
    slot_stiff = anchor_stiff[0][:, :, None]
    flat_rows = slot_rows.reshape(-1)

    def apply_operator(values):
        cable_part = values[:CABLE_ROWS]
        deck_part = values[CABLE_ROWS:]
        cable_flux = cable_links * (cable_part[:-1] - cable_part[1:])
        cable_side = jnp.pad(cable_flux, ((0, 1), (0, 0))) - jnp.pad(cable_flux, ((1, 0), (0, 0)))
        outgoing = jnp.take(values, slot_rows, axis=0, mode="fill", fill_value=0.0)
        incoming = lax.all_to_all(
            outgoing.astype(jnp.bfloat16), "rows", split_axis=0, concat_axis=0, tiled=True
        ).astype(outgoing.dtype)
        padded = with_halo(deck_part.astype(jnp.bfloat16), (("rows", 0),), 1).astype(
            deck_part.dtype
        )
        before_row = padded[0]
        after_row = padded[-1]
        deck_flux = deck_rigidity * (deck_part[:-1] - deck_part[1:])
        first_flux = left_open * (before_row - deck_part[0])
        last_flux = right_open * (deck_part[-1] - after_row)
        deck_side = jnp.concatenate([deck_flux, last_flux[None, :]], axis=0) - jnp.concatenate(
            [first_flux[None, :], deck_flux], axis=0
        )
        anchor_force = (slot_stiff * (outgoing - incoming)).reshape(-1, values.shape[1])
        anchor_side = jnp.zeros_like(values).at[flat_rows].add(anchor_force, mode="drop")
        springs = jnp.concatenate([cable_side, deck_side], axis=0)
        return node_mass[:, None] * values + springs + anchor_side

    start_block = vectors.astype(jnp.float32)
    center = (top_bound + cut_low) * 0.5
    half_width = (top_bound - cut_low) * 0.5
    first_degree = (apply_operator(start_block) - center * start_block) / half_width
    second_degree = (
        2.0 * (apply_operator(first_degree) - center * first_degree) / half_width - start_block
    )
    filtered = second_degree.astype(jnp.bfloat16)
    columns = lax.all_gather(filtered, "vecs", axis=1, tiled=True)
    total_rows = filtered.shape[0] * part_count
    gram_whole = jnp.einsum("rb,rc->bc", columns, columns, preferred_element_type=jnp.float32)
    gram_matrix = lax.psum(gram_whole, "rows") / total_rows
    lower_factor = jnp.linalg.cholesky(gram_matrix)
    identity = jnp.eye(gram_matrix.shape[0], dtype=jnp.float32)
    inverse = jax.scipy.linalg.solve_triangular(lower_factor, identity, lower=True)
    factor = inverse.T.astype(jnp.bfloat16)
    own_factor = lax.dynamic_slice_in_dim(factor, lax.axis_index("vecs") * own_width, own_width, 1)
    return jnp.dot(columns, own_factor, preferred_element_type=jnp.float32).astype(jnp.bfloat16)


def solution(mesh):
    return jax.shard_map(
        body,
        mesh=mesh,
        in_specs=(
            P("rows", "vecs"),
            P("rows"),
            P("rows"),
            P("rows", None),
            P(),
            P("rows", None, None),
            P("rows", None, None),
            P(),
            P(),
        ),
        out_specs=P("rows", "vecs"),
        check_vma=False,
    )
```

profile of v0, /device:TPU:3, one launch (start us, length us, event | category | flops | bytes accessed | tf_op | source)
XLA Modules:
  0.0 326.1 jit_solution(2909291328228950229)
XLA Ops:
  8.6 4.0 %collective-permute-start = (bf16[1,128]{1,0:T(2,128)(2,1)S(1)}, bf16[1,128]{1,0:T(2,128)(2,1)S(1)}, u32[]{:S(2)}, u32[]{:S(2)}) collective-permute-start(bf16[1,128]{1,0:T(2,128)(2,1)S(1)} %get-tuple-element.32), channel_id=1, source_target_pairs={{0,4},{4,8},{8,12},{12,16},{16,20},{20,24},{24,28},{1,5},{5,9},{9,... | collective-permute-start | bytes 776 | tf_op jit(solution)/shard_map/ppermute | solution.py:14
  15.4 5.4 %all-to-all-start = ((bf16[8,4,128]{2,1,0:T(4,128)(2,1)}), bf16[8,4,128]{2,1,0:T(4,128)(2,1)S(1)}, u32[]{:S(2)}, u32[]{:S(2)}) async-start(bf16[8,4,128]{2,1,0:T(4,128)(2,1)} %select_convert_fusion.1), calls=%async_computation | async-start | bytes 16384 | tf_op jit(solution)/shard_map/all_to_all | solution.py:52
  25.3 2.9 maximum_add_fusion
  28.3 3.3 %scatter_fusion = f32[3072,128]{1,0:T(8,128)} fusion(f32[3072,128]{1,0:T(8,128)} %maximum_add_fusion, s32[32]{0:T(128)S(1)} %fusion.37, f32[32,128]{1,0:T(8,128)S(1)} %bitcast.75), kind=kCustom, calls=%fused_computation.2 | custom fusion | flops 4096 | bytes 49280 | tf_op jit(solution)/shard_map/scatter-add | solution.py:67
  31.6 2.5 fusion.47
  38.1 4.0 %collective-permute-start.2 = (bf16[1,128]{1,0:T(2,128)(2,1)S(1)}, bf16[1,128]{1,0:T(2,128)(2,1)S(1)}, u32[]{:S(2)}, u32[]{:S(2)}) collective-permute-start(bf16[1,128]{1,0:T(2,128)(2,1)S(1)} %get-tuple-element.30), channel_id=1, source_target_pairs={{0,4},{4,8},{8,12},{12,16},{16,20},{20,24},{24,28},{1,5},{5,9},{9,... | collective-permute-start | bytes 776 | tf_op jit(solution)/shard_map/ppermute | solution.py:14
  42.1 2.8 pad_subtract_fusion
  46.5 5.4 %all-to-all-start.1 = ((bf16[8,4,128]{2,1,0:T(4,128)(2,1)}), bf16[8,4,128]{2,1,0:T(4,128)(2,1)S(1)}, u32[]{:S(2)}, u32[]{:S(2)}) async-start(bf16[8,4,128]{2,1,0:T(4,128)(2,1)} %select_convert_fusion), calls=%async_computation.1 | async-start | bytes 16384 | tf_op jit(solution)/shard_map/all_to_all | solution.py:52
  52.1 2.9 maximum_add_fusion.1
  55.0 2.3 all-to-all-done.1
  57.4 3.3 %scatter_fusion.1 = f32[3072,128]{1,0:T(8,128)} fusion(f32[3072,128]{1,0:T(8,128)} %maximum_add_fusion.1, s32[32]{0:T(128)S(1)} %fusion.37, f32[32,128]{1,0:T(8,128)S(1)} %bitcast.74), kind=kCustom, calls=%fused_computation.3 | custom fusion | flops 4096 | bytes 49280 | tf_op jit(solution)/shard_map/scatter-add | solution.py:67
  60.7 2.6 subtract_convert_fusion
  63.6 29.1 %all-gather.2.cloned.1.call-done = bf16[3072,512]{1,0:T(8,128)(2,1)} async-done(((bf16[3072,128]{1,0:T(8,128)(2,1)}), bf16[3072,512]{1,0:T(8,128)(2,1)}) %all-gather.2.cloned.1.call-update) | async-done | bytes 3145744 | tf_op jit(solution)/shard_map/all_gather | solution.py:79
  92.7 5.7 %fusion.54 = f32[512,512]{0,1:T(8,128)} fusion(bf16[3072,512]{1,0:T(8,128)(2,1)} %all-gather.2.cloned.1.call-done), kind=kOutput, calls=%fused_computation.131 | convolution fusion | flops 1610612736 | bytes 4194304 | tf_op jit(solution)/shard_map/rb,rc->bc/dot_general | solution.py:81
  99.6 77.9 %all-reduce.7.cloned.1.call-done = f32[512,512]{0,1:T(8,128)} async-done(((f32[512,512]{0,1:T(8,128)}), f32[512,512]{0,1:T(8,128)}) %all-reduce.7.cloned.1.call-update) | async-done | bytes 1048592 | tf_op jit(solution)/shard_map/psum | solution.py:82
  180.3 11.7 %cholesky.104 = f32[128,128]{1,0:T(8,128)S(1)} custom-call(f32[128,128]{1,0:T(8,128)S(1)} %cholesky.266), custom_call_target="Cholesky" | custom-call | tf_op jit(solution)/shard_map/jit(cholesky)/cholesky | solution.py:83
  192.1 9.8 %custom-call.31 = f32[1,128,128]{1,2,0:T(8,128)S(1)} custom-call(f32[1,128,128]{2,1,0:T(8,128)S(1)} %get-tuple-element.43), custom_call_target="InvertDiagBlocksLowerTriangular" | custom-call | tf_op jit(solution)/shard_map/jit(cholesky)/cholesky | solution.py:83
  202.6 11.9 %cholesky.217 = f32[128,128]{1,0:T(8,128)S(1)} custom-call(f32[128,128]{1,0:T(8,128)S(1)} %cholesky.270), custom_call_target="Cholesky" | custom-call | tf_op jit(solution)/shard_map/jit(cholesky)/cholesky | solution.py:83
  214.6 9.8 %custom-call.32 = f32[1,128,128]{1,2,0:T(8,128)S(1)} custom-call(f32[1,128,128]{2,1,0:T(8,128)S(1)} %get-tuple-element.40), custom_call_target="InvertDiagBlocksLowerTriangular" | custom-call | tf_op jit(solution)/shard_map/jit(cholesky)/cholesky | solution.py:83
  225.1 11.7 %cholesky.238 = f32[128,128]{1,0:T(8,128)S(1)} custom-call(f32[128,128]{1,0:T(8,128)S(1)} %cholesky.275), custom_call_target="Cholesky" | custom-call | tf_op jit(solution)/shard_map/jit(cholesky)/cholesky | solution.py:83
  236.8 9.8 %custom-call.33 = f32[1,128,128]{1,2,0:T(8,128)S(1)} custom-call(f32[1,128,128]{2,1,0:T(8,128)S(1)} %get-tuple-element.37), custom_call_target="InvertDiagBlocksLowerTriangular" | custom-call | tf_op jit(solution)/shard_map/jit(cholesky)/cholesky | solution.py:83
  247.2 11.9 %cholesky.255 = f32[128,128]{1,0:T(8,128)S(1)} custom-call(f32[128,128]{1,0:T(8,128)S(1)} %convolution_subtract_fusion.5), custom_call_target="Cholesky" | custom-call | tf_op jit(solution)/shard_map/jit(cholesky)/cholesky | solution.py:83
  263.7 9.7 %while.1 = (s32[]{:T(128)}, f32[512,512]{1,0:T(8,128)S(1)}, s32[4,2]{0,1:T(2,128)S(1)}, f32[4,128,128]{2,1,0:T(8,128)}, s32[]{:T(128)}) while((s32[]{:T(128)}, f32[512,512]{1,0:T(8,128)S(1)}, s32[4,2]{0,1:T(2,128)S(1)}, f32[4,128,128]{2,1,0:T(8,128)}, s32[]{:T(128)}) %tuple.36), condition=%wide.while_cond, body=%wide.while_body.sunk | while | flops 2 | bytes 132205 | solution.py:85
  273.5 40.1 %custom-call.34 = f32[4,128,128]{1,2,0:T(8,128)S(1)} custom-call(f32[4,128,128]{2,1,0:T(8,128)} %get-tuple-element.13), custom_call_target="InvertDiagBlocksLowerTriangular" | custom-call | tf_op jit(solution)/shard_map/jit(_solve_triangular)/triangular_solve | solution.py:85
  (110 shorter events, 36.4 us)
Async XLA Ops:
  6.5 7.3 %copy-start.5 = (s32[1,8,4]{1,2,0:T(4,128)S(1)}, s32[1,8,4]{1,2,0:T(4,128)}, u32[]{:S(2)}) copy-start(s32[1,8,4]{1,2,0:T(4,128)} %param.16) | copy-start | bytes 388
  7.3 17.7 %collective-permute-start.1 = (bf16[1,128]{1,0:T(2,128)(2,1)S(1)}, bf16[1,128]{1,0:T(2,128)(2,1)S(1)}, u32[]{:S(2)}, u32[]{:S(2)}) collective-permute-start(bf16[1,128]{1,0:T(2,128)(2,1)S(1)} %get-tuple-element.33), channel_id=1, source_target_pairs={{4,0},{8,4},{12,8},{16,12},{20,16},{24,20},{28,24},{5,1},{9,5},{13... | collective-permute-start | bytes 776 | tf_op jit(solution)/shard_map/ppermute | solution.py:17
  8.5 14.4 %copy-start.8 = (s32[1,4]{1,0:T(1,128)S(1)}, s32[1,4]{1,0:T(1,128)}, u32[]{:S(2)}) copy-start(s32[1,4]{1,0:T(1,128)} %param.14) | copy-start | bytes 52
  8.6 14.7 %copy-start.6 = (f32[3072]{0:T(1024)S(1)}, f32[3072]{0:T(1024)}, u32[]{:S(2)}) copy-start(f32[3072]{0:T(1024)} %param.13) | copy-start | bytes 36868
  8.6 16.4 %collective-permute-start = (bf16[1,128]{1,0:T(2,128)(2,1)S(1)}, bf16[1,128]{1,0:T(2,128)(2,1)S(1)}, u32[]{:S(2)}, u32[]{:S(2)}) collective-permute-start(bf16[1,128]{1,0:T(2,128)(2,1)S(1)} %get-tuple-element.32), channel_id=1, source_target_pairs={{0,4},{4,8},{8,12},{12,16},{16,20},{20,24},{24,28},{1,5},{5,9},{9,... | collective-permute-start | bytes 776 | tf_op jit(solution)/shard_map/ppermute | solution.py:14
  15.4 12.8 %all-to-all-start = ((bf16[8,4,128]{2,1,0:T(4,128)(2,1)}), bf16[8,4,128]{2,1,0:T(4,128)(2,1)S(1)}, u32[]{:S(2)}, u32[]{:S(2)}) async-start(bf16[8,4,128]{2,1,0:T(4,128)(2,1)} %select_convert_fusion.1), calls=%async_computation | async-start | bytes 16384 | tf_op jit(solution)/shard_map/all_to_all | solution.py:52
  23.6 1.3 copy-start.7
  23.6 1.4 slice-start
  23.6 1.6 copy-start
  23.7 1.6 copy-start.4
  36.8 15.2 %collective-permute-start.3 = (bf16[1,128]{1,0:T(2,128)(2,1)S(1)}, bf16[1,128]{1,0:T(2,128)(2,1)S(1)}, u32[]{:S(2)}, u32[]{:S(2)}) collective-permute-start(bf16[1,128]{1,0:T(2,128)(2,1)S(1)} %get-tuple-element.31), channel_id=1, source_target_pairs={{4,0},{8,4},{12,8},{16,12},{20,16},{24,20},{28,24},{5,1},{9,5},{13... | collective-permute-start | bytes 776 | tf_op jit(solution)/shard_map/ppermute | solution.py:17
  38.1 13.9 %collective-permute-start.2 = (bf16[1,128]{1,0:T(2,128)(2,1)S(1)}, bf16[1,128]{1,0:T(2,128)(2,1)S(1)}, u32[]{:S(2)}, u32[]{:S(2)}) collective-permute-start(bf16[1,128]{1,0:T(2,128)(2,1)S(1)} %get-tuple-element.30), channel_id=1, source_target_pairs={{0,4},{4,8},{8,12},{12,16},{16,20},{20,24},{24,28},{1,5},{5,9},{9,... | collective-permute-start | bytes 776 | tf_op jit(solution)/shard_map/ppermute | solution.py:14
  46.5 10.8 %all-to-all-start.1 = ((bf16[8,4,128]{2,1,0:T(4,128)(2,1)}), bf16[8,4,128]{2,1,0:T(4,128)(2,1)S(1)}, u32[]{:S(2)}, u32[]{:S(2)}) async-start(bf16[8,4,128]{2,1,0:T(4,128)(2,1)} %select_convert_fusion), calls=%async_computation.1 | async-start | bytes 16384 | tf_op jit(solution)/shard_map/all_to_all | solution.py:52
  51.9 40.7 %all-gather.2.cloned.1.call-start = ((), (), s32[]{:S(2)}) async-start(), calls=%async_computation.2 | async-start | bytes 3932160 | tf_op jit(solution)/shard_map/all_gather | solution.py:79
  63.3 114.1 %all-reduce.7.cloned.1.call-start = ((), (), s32[]{:S(2)}) async-start(), calls=%async_computation.3 | async-start | bytes 2097152 | tf_op jit(solution)/shard_map/psum | solution.py:82
  178.8 1.2 copy-start.2
  263.6 50.4 %copy-start.3 = (f32[512,512]{1,0:T(8,128)S(1)}, f32[512,512]{1,0:T(8,128)}, u32[]{:S(2)}) copy-start(f32[512,512]{1,0:T(8,128)} %fusion.13) | copy-start | bytes 3145732
  314.7 1.9 copy-start.1
Sparse Core Ops, SparseCore 0:
  63.5 29.1 all-gather.1
  98.5 78.8 all-reduce.6
where the time goes:
time: 332 us; the launch traced here: 326 us
  other arithmetic  148 us (45%)
  waiting for transfers between devices  109 us (33%)
  starting transfers between devices  21.7 us (7%)
  between operations  18.7 us (6%)
  local copies, waits for them, and re-layouts  15.4 us (5%)
  matrix products  12.6 us (4%)
    another operation x14, other arithmetic, body(): lower_factor = jnp.linalg.cholesky(gram_matrix)  78.8 us
    psum x1, waiting for transfers between devices, body(): gram_matrix = lax.psum(gram_whole, 'rows') / total_rows  77.9 us
    another operation x3, other arithmetic, body(): jax.scipy.linalg.solve_triangular(lower_factor, identity, lower=True)  40.3 us
    all_gather x1, waiting for transfers between devices, body(): columns = lax.all_gather(filtered, 'vecs', axis=1, tiled=True)  29.1 us
    all_to_all x2, starting transfers between devices, apply_operator(): lax.all_to_all(outgoing.astype(jnp.bfloat16), 'rows', split_axis=0, conca...  10.9 us
    another operation x12, local copies, waits for them, and re-layouts  9.73 us
    ppermute x2, starting transfers between devices, with_halo(): lax.ppermute(lax.slice_in_dim(block, block.shape[dim] - width, None, axis...  7.98 us
  transfers between devices with their start and end apart: 8, of which 3 were waited for; matrix products, arithmetic and copies ran while one was open for 5% of the time, Pallas kernels for 0%

commit v1 on v0

--- a/solution.py
+++ b/solution.py
@@ -1,9 +1,67 @@
 import jax
 import jax.numpy as jnp
 from jax import lax
+from jax.experimental import pallas as pl
+from jax.experimental.pallas import tpu as pltpu
 from jax.sharding import PartitionSpec as P
 
 CABLE_ROWS = 2304
+NB = 128
+HI = lax.Precision.HIGHEST
+
+
+def eliminate(block):
+    lane = lax.broadcasted_iota(jnp.int32, (8, NB), 1)
+    sub = lax.broadcasted_iota(jnp.int32, (8, NB), 0)
+    tiles = NB // 8
+    left = [block[8 * t : 8 * t + 8, :] for t in range(tiles)]
+    right = [jnp.where(lane == sub + 8 * t, 1.0, 0.0).astype(jnp.float32) for t in range(tiles)]
+    for j in range(NB):
+        home, row = divmod(j, 8)
+        pivot_row = left[home][row : row + 1, :]
+        scale = lax.rsqrt(pivot_row[:, j : j + 1])
+        scaled = pivot_row * scale
+        inverse_row = right[home][row : row + 1, :] * scale
+        scaled_all = jnp.broadcast_to(scaled, (8, NB))
+        inverse_all = jnp.broadcast_to(inverse_row, (8, NB))
+        for t in range(home, tiles):
+            column = jnp.broadcast_to(left[t][:, j : j + 1], (8, NB)) * scale
+            if t == home:
+                below = sub > row
+                left[t] = jnp.where(below, left[t] - column * scaled_all, left[t])
+                right[t] = jnp.where(
+                    below, right[t] - column * inverse_all, jnp.where(sub == row, inverse_all, right[t])
+                )
+            else:
+                left[t] = left[t] - column * scaled_all
+                right[t] = right[t] - column * inverse_all
+    return jnp.concatenate(right, axis=0)
+
+
+def mm(a, b, dims):
+    return lax.dot_general(a, b, (dims, ((), ())), precision=HI, preferred_element_type=jnp.float32)
+
+
+def inverse_factor(gram_ref, inv_ref):
+    size = gram_ref.shape[0]
+    inv_ref[...] = jnp.zeros_like(inv_ref)
+    for k in range(size // NB):
+        lo, hi = k * NB, (k + 1) * NB
+        diag_inv = eliminate(gram_ref[lo:hi, lo:hi])
+        if k:
+            inv_ref[lo:hi, :lo] = mm(diag_inv, inv_ref[lo:hi, :lo], ((1,), (0,)))
+        inv_ref[lo:hi, lo:hi] = diag_inv
+        if hi < size:
+            panel = mm(gram_ref[hi:, lo:hi], diag_inv, ((1,), (1,)))
+            for i in range(hi, size, NB):
+                part = panel[i - hi : i - hi + NB]
+                gram_ref[i : i + NB, hi : i + NB] -= mm(part, panel[: i - hi + NB], ((1,), (1,)))
+            inv_ref[hi:, :hi] -= mm(panel, inv_ref[lo:hi, :hi], ((1,), (0,)))
+
+
+def inverse_kernel(gram_in, out, gram_ref):
+    gram_ref[...] = gram_in[...]
+    inverse_factor(gram_ref, out)
 
 
 def with_halo(block, sides, width):
@@ -80,9 +138,14 @@
     total_rows = filtered.shape[0] * part_count
     gram_whole = jnp.einsum("rb,rc->bc", columns, columns, preferred_element_type=jnp.float32)
     gram_matrix = lax.psum(gram_whole, "rows") / total_rows
-    lower_factor = jnp.linalg.cholesky(gram_matrix)
-    identity = jnp.eye(gram_matrix.shape[0], dtype=jnp.float32)
-    inverse = jax.scipy.linalg.solve_triangular(lower_factor, identity, lower=True)
+    size = gram_matrix.shape[0]
+    inverse = pl.pallas_call(
+        inverse_kernel,
+        out_shape=jax.ShapeDtypeStruct((size, size), jnp.float32),
+        in_specs=[pl.BlockSpec(memory_space=pltpu.VMEM)],
+        out_specs=pl.BlockSpec(memory_space=pltpu.VMEM),
+        scratch_shapes=[pltpu.VMEM((size, size), jnp.float32)],
+    )(gram_matrix)
     factor = inverse.T.astype(jnp.bfloat16)
     own_factor = lax.dynamic_slice_in_dim(factor, lax.axis_index("vecs") * own_width, own_width, 1)
     return jnp.dot(columns, own_factor, preferred_element_type=jnp.float32).astype(jnp.bfloat16)

time: 332 us -> 261 us (0.79); the launches traced: 326 us -> 259 us
  other arithmetic: 148 us -> 27.2 us
  Pallas kernels: 0 us -> 72.5 us
  local copies, waits for them, and re-layouts: 15.4 us -> 2.75 us
  matrix products: 12.6 us -> 8.43 us
    another operation x19 -> x2, other arithmetic: 122 us -> 1.84 us  [the longest x14 78.8 us: body(): lower_factor = jnp.linalg.cholesky(gram_matrix)]
    pallas_call x0 -> x1, Pallas kernels: none -> 72.5 us  [body(): pl.pallas_call(inverse_kernel, out_shape=jax.ShapeDtypeStruct((size, size...]
    another operation x17 -> x0, local copies, waits for them, and re-layouts: 9.87 us -> none
    another operation x13 -> x0, matrix products: 4.88 us -> none  [the longest x7 3.01 us: body(): jax.scipy.linalg.solve_triangular(lower_factor, identity, lower=True)]
where the time goes in v1:
time: 261 us; the launch traced here: 259 us
  waiting for transfers between devices  111 us (43%)
  Pallas kernels  72.5 us (28%)
  other arithmetic  27.2 us (10%)
  starting transfers between devices  21.8 us (8%)
  between operations  15.6 us (6%)
  matrix products  8.43 us (3%)
  local copies, waits for them, and re-layouts  2.75 us (1%)
    psum x1, waiting for transfers between devices, body(): gram_matrix = lax.psum(gram_whole, 'rows') / total_rows  79.1 us
    pallas_call x1, Pallas kernels, body(): pl.pallas_call(inverse_kernel, out_shape=jax.ShapeDtypeStruct((size, size...  72.5 us
    all_gather x1, waiting for transfers between devices, body(): columns = lax.all_gather(filtered, 'vecs', axis=1, tiled=True)  29.7 us
    all_to_all x2, starting transfers between devices, apply_operator(): lax.all_to_all(outgoing.astype(jnp.bfloat16), 'rows', split_axis=0, conca...  12.5 us
    scatter-add x2, other arithmetic, apply_operator(): jnp.zeros_like(values).at[flat_rows].add(anchor_force, mode='drop')  6.51 us
    ppermute x2, starting transfers between devices, with_halo(): lax.ppermute(lax.slice_in_dim(block, block.shape[dim] - width, None, axis...  6.48 us
    dot_general x1, matrix products, body(): jnp.einsum('rb,rc->bc', columns, columns, preferred_element_type=jnp.floa...  5.62 us
  transfers between devices with their start and end apart: 8, of which 3 were waited for; matrix products, arithmetic and copies ran while one was open for 5% of the time, Pallas kernels for 0%

profile of v1, /device:TPU:3, one launch (start us, length us, event | category | flops | bytes accessed | tf_op | source)
XLA Modules:
  0.0 258.8 jit_solution(18360703555270361308)
XLA Ops:
  6.5 0.7 fusion.14
  7.3 3.1 %collective-permute-start = (bf16[1,128]{1,0:T(2,128)(2,1)S(1)}, bf16[1,128]{1,0:T(2,128)(2,1)S(1)}, u32[]{:S(2)}, u32[]{:S(2)}) collective-permute-start(bf16[1,128]{1,0:T(2,128)(2,1)S(1)} %get-tuple-element.14), channel_id=1, source_target_pairs={{0,4},{4,8},{8,12},{12,16},{16,20},{20,24},{24,28},{1,5},{5,9},{9,... | collective-permute-start | bytes 776 | tf_op jit(solution)/shard_map/ppermute | solution.py:72
  10.4 1.3 collective-permute-start.1
  13.1 1.2 convert_element_type.39
  15.9 6.4 %all-to-all-start = ((bf16[8,4,128]{2,1,0:T(4,128)(2,1)}), bf16[8,4,128]{2,1,0:T(4,128)(2,1)S(1)}, u32[]{:S(2)}, u32[]{:S(2)}) async-start(bf16[8,4,128]{2,1,0:T(4,128)(2,1)} %select_convert_fusion.1), calls=%async_computation | async-start | bytes 16384 | tf_op jit(solution)/shard_map/all_to_all | solution.py:110
  25.2 1.1 pad_subtract_fusion.1
  26.8 2.9 %maximum_add_fusion = f32[3072,128]{1,0:T(8,128)} fusion(f32[768,128]{1,0:T(8,128)S(1)} %maximum_subtract_fusion, f32[2304,128]{1,0:T(8,128)} %pad_subtract_fusion.1, bf16[3072,128]{1,0:T(8,128)(2,1)S(1)} %copy-done, f32[3072]{0:T(1024)S(1)} %copy-done.2), kind=kLoop, calls=%fused_computation.5 | loop fusion | flops 1572864 | bytes 3944448 | tf_op jit(solution)/shard_map/add | solution.py:127
  29.8 3.3 %scatter_fusion = f32[3072,128]{1,0:T(8,128)} fusion(f32[3072,128]{1,0:T(8,128)} %maximum_add_fusion, s32[32]{0:T(128)S(1)} %fusion.4, f32[32,128]{1,0:T(8,128)S(1)} %bitcast.21), kind=kCustom, calls=%fused_computation.2 | custom fusion | flops 4096 | bytes 49280 | tf_op jit(solution)/shard_map/scatter-add | solution.py:125
  33.1 1.7 fusion.12
  35.3 1.4 fusion
  36.7 3.4 %collective-permute-start.2 = (bf16[1,128]{1,0:T(2,128)(2,1)S(1)}, bf16[1,128]{1,0:T(2,128)(2,1)S(1)}, u32[]{:S(2)}, u32[]{:S(2)}) collective-permute-start(bf16[1,128]{1,0:T(2,128)(2,1)S(1)} %get-tuple-element.12), channel_id=1, source_target_pairs={{0,4},{4,8},{8,12},{12,16},{16,20},{20,24},{24,28},{1,5},{5,9},{9,... | collective-permute-start | bytes 776 | tf_op jit(solution)/shard_map/ppermute | solution.py:72
  40.1 1.3 collective-permute-start.3
  42.1 6.1 %all-to-all-start.1 = ((bf16[8,4,128]{2,1,0:T(4,128)(2,1)}), bf16[8,4,128]{2,1,0:T(4,128)(2,1)S(1)}, u32[]{:S(2)}, u32[]{:S(2)}) async-start(bf16[8,4,128]{2,1,0:T(4,128)(2,1)} %select_convert_fusion), calls=%async_computation.1 | async-start | bytes 16384 | tf_op jit(solution)/shard_map/all_to_all | solution.py:110
  48.2 1.8 pad_subtract_fusion
  50.1 1.6 maximum_add_fusion.1
  51.7 1.8 all-to-all-done.1
  53.6 3.3 %scatter_fusion.1 = f32[3072,128]{1,0:T(8,128)} fusion(f32[3072,128]{1,0:T(8,128)} %maximum_add_fusion.1, s32[32]{0:T(128)S(1)} %fusion.4, f32[32,128]{1,0:T(8,128)S(1)} %bitcast.20), kind=kCustom, calls=%fused_computation.3 | custom fusion | flops 4096 | bytes 49280 | tf_op jit(solution)/shard_map/scatter-add | solution.py:125
  56.8 2.6 %subtract_convert_fusion = bf16[3072,128]{1,0:T(8,128)(2,1)} fusion(f32[3072,128]{1,0:T(8,128)} %scatter_fusion.1, f32[3072,128]{1,0:T(8,128)S(1)} %get-tuple-element.7, bf16[3072,128]{1,0:T(8,128)(2,1)S(1)} %copy-done, f32[]{:T(128)S(6)} %mul.119, f32[]{:T(128)S(6)} %mul.116), kind=kLoop, calls=%fused_computation.7 | loop fusion | flops 2752512 | bytes 4718600 | tf_op jit(solution)/shard_map/convert_element_type | solution.py:136
  59.7 29.7 %all-gather.2.cloned.1.call-done = bf16[3072,512]{1,0:T(8,128)(2,1)} async-done(((bf16[3072,128]{1,0:T(8,128)(2,1)}), bf16[3072,512]{1,0:T(8,128)(2,1)}) %all-gather.2.cloned.1.call-update) | async-done | bytes 3145744 | tf_op jit(solution)/shard_map/all_gather | solution.py:137
  89.4 5.6 %fusion.15 = f32[512,512]{1,0:T(8,128)} fusion(bf16[3072,512]{1,0:T(8,128)(2,1)} %all-gather.2.cloned.1.call-done), kind=kOutput, calls=%fused_computation.53 | convolution fusion | flops 1610612736 | bytes 4194304 | tf_op jit(solution)/shard_map/rb,rc->bc/dot_general | solution.py:139
  95.1 79.1 %all-reduce.6.cloned.1.call-done = f32[512,512]{1,0:T(8,128)} async-done(((f32[512,512]{1,0:T(8,128)}), f32[512,512]{1,0:T(8,128)}) %all-reduce.6.cloned.1.call-update) | async-done | bytes 1048592 | tf_op jit(solution)/shard_map/psum | solution.py:140
  174.2 2.5 broadcast_multiply_fusion.gram_in
  176.7 72.5 %shard_map.91 = f32[512,512]{1,0:T(8,128)} custom-call(f32[512,512]{1,0:T(8,128)} %broadcast_multiply_fusion.gram_in), custom_call_target="tpu_custom_call" | custom-call | tf_op jit(solution)/shard_map/pallas_call | solution.py:142
  249.2 2.8 %convolution_convert_fusion = bf16[3072,128]{1,0:T(8,128)(2,1)} fusion(bf16[3072,512]{1,0:T(8,128)(2,1)S(1)} %copy-done.1, f32[512,512]{1,0:T(8,128)} %shard_map.91, s32[]{:T(128)S(6)} %select_n.36), kind=kOutput, calls=%fused_computation.4 | convolution fusion | flops 403046400 | bytes 4063236 | tf_op jit(solution)/shard_map/dot_general | solution.py:151
  (54 shorter events, 6.1 us)
Async XLA Ops:
  6.5 17.0 %copy-start.3 = (s32[1,8,4]{1,2,0:T(4,128)S(1)}, s32[1,8,4]{1,2,0:T(4,128)}, u32[]{:S(2)}) copy-start(s32[1,8,4]{1,2,0:T(4,128)} %param.16) | copy-start | bytes 388
  6.5 17.8 %copy-start.6 = (s32[1,4]{1,0:T(1,128)S(1)}, s32[1,4]{1,0:T(1,128)}, u32[]{:S(2)}) copy-start(s32[1,4]{1,0:T(1,128)} %param.14) | copy-start | bytes 52
  7.3 19.1 %collective-permute-start = (bf16[1,128]{1,0:T(2,128)(2,1)S(1)}, bf16[1,128]{1,0:T(2,128)(2,1)S(1)}, u32[]{:S(2)}, u32[]{:S(2)}) collective-permute-start(bf16[1,128]{1,0:T(2,128)(2,1)S(1)} %get-tuple-element.14), channel_id=1, source_target_pairs={{0,4},{4,8},{8,12},{12,16},{16,20},{20,24},{24,28},{1,5},{5,9},{9,... | collective-permute-start | bytes 776 | tf_op jit(solution)/shard_map/ppermute | solution.py:72
  10.4 16.0 %collective-permute-start.1 = (bf16[1,128]{1,0:T(2,128)(2,1)S(1)}, bf16[1,128]{1,0:T(2,128)(2,1)S(1)}, u32[]{:S(2)}, u32[]{:S(2)}) collective-permute-start(bf16[1,128]{1,0:T(2,128)(2,1)S(1)} %get-tuple-element.15), channel_id=1, source_target_pairs={{4,0},{8,4},{12,8},{16,12},{20,16},{24,20},{28,24},{5,1},{9,5},{13... | collective-permute-start | bytes 776 | tf_op jit(solution)/shard_map/ppermute | solution.py:75
  13.1 11.7 %copy-start.4 = (f32[3072]{0:T(1024)S(1)}, f32[3072]{0:T(1024)}, u32[]{:S(2)}) copy-start(f32[3072]{0:T(1024)} %param.13) | copy-start | bytes 36868
  15.9 13.9 %all-to-all-start = ((bf16[8,4,128]{2,1,0:T(4,128)(2,1)}), bf16[8,4,128]{2,1,0:T(4,128)(2,1)S(1)}, u32[]{:S(2)}, u32[]{:S(2)}) async-start(bf16[8,4,128]{2,1,0:T(4,128)(2,1)} %select_convert_fusion.1), calls=%async_computation | async-start | bytes 16384 | tf_op jit(solution)/shard_map/all_to_all | solution.py:110
  25.1 1.2 copy-start.5
  25.2 1.3 slice-start
  25.2 1.6 copy-start
  25.2 1.6 copy-start.2
  36.7 13.3 %collective-permute-start.2 = (bf16[1,128]{1,0:T(2,128)(2,1)S(1)}, bf16[1,128]{1,0:T(2,128)(2,1)S(1)}, u32[]{:S(2)}, u32[]{:S(2)}) collective-permute-start(bf16[1,128]{1,0:T(2,128)(2,1)S(1)} %get-tuple-element.12), channel_id=1, source_target_pairs={{0,4},{4,8},{8,12},{12,16},{16,20},{20,24},{24,28},{1,5},{5,9},{9,... | collective-permute-start | bytes 776 | tf_op jit(solution)/shard_map/ppermute | solution.py:72
  40.1 9.9 %collective-permute-start.3 = (bf16[1,128]{1,0:T(2,128)(2,1)S(1)}, bf16[1,128]{1,0:T(2,128)(2,1)S(1)}, u32[]{:S(2)}, u32[]{:S(2)}) collective-permute-start(bf16[1,128]{1,0:T(2,128)(2,1)S(1)} %get-tuple-element.13), channel_id=1, source_target_pairs={{4,0},{8,4},{12,8},{16,12},{20,16},{24,20},{28,24},{5,1},{9,5},{13... | collective-permute-start | bytes 776 | tf_op jit(solution)/shard_map/ppermute | solution.py:75
  42.1 11.4 %all-to-all-start.1 = ((bf16[8,4,128]{2,1,0:T(4,128)(2,1)}), bf16[8,4,128]{2,1,0:T(4,128)(2,1)S(1)}, u32[]{:S(2)}, u32[]{:S(2)}) async-start(bf16[8,4,128]{2,1,0:T(4,128)(2,1)} %select_convert_fusion), calls=%async_computation.1 | async-start | bytes 16384 | tf_op jit(solution)/shard_map/all_to_all | solution.py:110
  48.1 41.3 %all-gather.2.cloned.1.call-start = ((), (), s32[]{:S(2)}) async-start(), calls=%async_computation.2 | async-start | bytes 3932160 | tf_op jit(solution)/shard_map/all_gather | solution.py:137
  59.5 114.7 %all-reduce.6.cloned.1.call-start = ((), (), s32[]{:S(2)}) async-start(), calls=%async_computation.3 | async-start | bytes 2097152 | tf_op jit(solution)/shard_map/psum | solution.py:140
  174.2 75.0 %copy-start.1 = (bf16[3072,512]{1,0:T(8,128)(2,1)S(1)}, bf16[3072,512]{1,0:T(8,128)(2,1)}, u32[]{:S(2)}) copy-start(bf16[3072,512]{1,0:T(8,128)(2,1)} %all-gather.2.cloned.1.call-done) | copy-start | bytes 9437188
Sparse Core Ops, SparseCore 0:
  59.6 29.7 all-gather.1
  95.2 78.9 all-reduce.5

commit v2 on v1

v2 whole, which is shorter than its diff:
```python
import functools

import jax
import jax.numpy as jnp
from jax import lax
from jax.experimental import pallas as pl
from jax.experimental.pallas import tpu as pltpu
from jax.sharding import PartitionSpec as P

CABLE_ROWS = 2304
MESH = pl.DeviceIdType.MESH
PAD = 8

NB = 128
HI = lax.Precision.HIGHEST


def eliminate(block):
    lane = lax.broadcasted_iota(jnp.int32, (8, NB), 1)
    sub = lax.broadcasted_iota(jnp.int32, (8, NB), 0)
    tiles = NB // 8
    left = [block[8 * t : 8 * t + 8, :] for t in range(tiles)]
    right = [jnp.where(lane == sub + 8 * t, 1.0, 0.0).astype(jnp.float32) for t in range(tiles)]
    for j in range(NB):
        home, row = divmod(j, 8)
        pivot_row = left[home][row : row + 1, :]
        scale = lax.rsqrt(pivot_row[:, j : j + 1])
        scaled = pivot_row * scale
        inverse_row = right[home][row : row + 1, :] * scale
        scaled_all = jnp.broadcast_to(scaled, (8, NB))
        inverse_all = jnp.broadcast_to(inverse_row, (8, NB))
        for t in range(home, tiles):
            column = jnp.broadcast_to(left[t][:, j : j + 1], (8, NB)) * scale
            if t == home:
                below = sub > row
                left[t] = jnp.where(below, left[t] - column * scaled_all, left[t])
                right[t] = jnp.where(
                    below, right[t] - column * inverse_all, jnp.where(sub == row, inverse_all, right[t])
                )
            else:
                left[t] = left[t] - column * scaled_all
                right[t] = right[t] - column * inverse_all
    return jnp.concatenate(right, axis=0)


def mm(a, b, dims):
    return lax.dot_general(a, b, (dims, ((), ())), precision=HI, preferred_element_type=jnp.float32)


def inverse_factor(gram_ref, inv_ref):
    size = gram_ref.shape[0]
    inv_ref[...] = jnp.zeros_like(inv_ref)
    for k in range(size // NB):
        lo, hi = k * NB, (k + 1) * NB
        diag_inv = eliminate(gram_ref[lo:hi, lo:hi])
        if k:
            inv_ref[lo:hi, :lo] = mm(diag_inv, inv_ref[lo:hi, :lo], ((1,), (0,)))
        inv_ref[lo:hi, lo:hi] = diag_inv
        if hi < size:
            panel = mm(gram_ref[hi:, lo:hi], diag_inv, ((1,), (1,)))
            for i in range(hi, size, NB):
                part = panel[i - hi : i - hi + NB]
                gram_ref[i : i + NB, hi : i + NB] -= mm(part, panel[: i - hi + NB], ((1,), (1,)))
            inv_ref[hi:, :hi] -= mm(panel, inv_ref[lo:hi, :hi], ((1,), (0,)))


def split_three(value):
    high = value.astype(jnp.bfloat16)
    rest = value - high.astype(jnp.float32)
    middle = rest.astype(jnp.bfloat16)
    low = (rest - middle.astype(jnp.float32)).astype(jnp.bfloat16)
    return jnp.concatenate([high, middle, low], axis=0)


def kernel(
    parts,
    splits,
    x_ref,
    mass_ref,
    stiff_ref,
    nodes_ref,
    rigid_ref,
    rows_ref,
    spring_ref,
    low_ref,
    top_ref,
    target_ref,
    out_ref,
    value_ref,
    first_ref,
    link_ref,
    diag_ref,
    hot_ref,
    force_ref,
    send_buf,
    recv_buf,
    cols_ref,
    sum_ref,
    half_ref,
    piece_ref,
    all_ref,
    gram_ref,
    inv_ref,
    ex_send,
    ex_recv,
    quarter_send,
    quarter_recv,
    fold_send,
    fold_recv,
    piece_send,
    piece_recv,
    give_send,
    give_recv,
    grow_send,
    grow_recv,
):
    me = lax.axis_index("rows")
    col = lax.axis_index("vecs")
    count, width = x_ref.shape
    slots = rows_ref.shape[1]
    total_rows = count * parts

    barrier = pltpu.get_barrier_semaphore()
    for k in range(1, splits):
        pl.semaphore_signal(
            barrier, inc=1, device_id=(me, lax.rem(col + k, splits)), device_id_type=MESH
        )

    def greet(k, carry):
        pl.semaphore_signal(
            barrier, inc=1, device_id=(lax.rem(me + k, parts), col), device_id_type=MESH
        )
        return carry

    lax.fori_loop(1, parts, greet, 0)
    pl.semaphore_wait(barrier, parts - 1 + splits - 1)

    top = jnp.full((1, width), top_ref[0], jnp.float32)
    bottom = jnp.full((1, width), low_ref[0], jnp.float32)
    center = (top + bottom) * 0.5
    inverse_half = 1.0 / ((top - bottom) * 0.5)

    chunk = count // splits
    zero_pad = jnp.zeros((PAD, width), jnp.float32)
    for ref in (value_ref, first_ref, link_ref):
        ref[0:PAD, :] = zero_pad
        ref[PAD + count :, :] = zero_pad
    for lo in range(0, count, chunk):
        value_ref[PAD + lo : PAD + lo + chunk, :] = x_ref[lo : lo + chunk, :].astype(jnp.float32)

    def remote(turn, k, target):
        return pltpu.make_async_remote_copy(
            src_ref=send_buf.at[turn, target],
            dst_ref=recv_buf.at[turn, me],
            send_sem=ex_send.at[turn, k],
            recv_sem=ex_recv.at[turn, k],
            device_id=(target, col),
            device_id_type=MESH,
        )

    def arrival(turn, k):
        source = lax.rem(me + parts - k, parts)
        return pltpu.make_async_remote_copy(
            src_ref=send_buf.at[turn, source],
            dst_ref=recv_buf.at[turn, source],
            send_sem=ex_send.at[turn, k],
            recv_sem=ex_recv.at[turn, k],
            device_id=(source, col),
            device_id_type=MESH,
        )

    unroll = parts <= 8

    def send_anchors(turn, ref):
        first_row = ref[PAD + CABLE_ROWS : PAD + CABLE_ROWS + 1, :]
        last_row = ref[PAD + count - 1 : PAD + count, :]
        blank = jnp.zeros((8 - slots - 2, width), jnp.float32)

        def pick(q, carry):
            picked = [
                ref[pl.ds(PAD + jnp.minimum(rows_ref[q, s], count - 1), 1), :] for s in range(slots)
            ]
            send_buf[turn, q] = jnp.concatenate(picked + [first_row, last_row, blank], axis=0)
            return carry

        lax.fori_loop(0, parts, pick, 0, unroll=unroll)

        def push(k, carry):
            remote(turn, k, lax.rem(me + k, parts)).start()
            return carry

        lax.fori_loop(1, parts, push, 0, unroll=unroll)
        recv_buf[turn, me] = send_buf[turn, me]

    def collect(turn, scale):
        def take(k, carry):
            arrival(turn, k).wait_recv()
            return carry

        lax.fori_loop(1, parts, take, 0, unroll=unroll)

        def pull(q, carry):
            difference = send_buf[turn, q] - recv_buf[turn, q]
            for s in range(slots):
                live = jnp.where(rows_ref[q, s] < count, spring_ref[q, s], 0.0)
                force_ref[pl.ds(q * slots + s, 1), :] = live * difference[s : s + 1, :]
            return carry

        lax.fori_loop(0, parts, pull, 0, unroll=unroll)
        before = recv_buf[turn, lax.rem(me + parts - 1, parts)]
        after = recv_buf[turn, lax.rem(me + 1, parts)]
        own = send_buf[turn, me]
        left_open = jnp.where(me > 0, rigid_ref[0], 0.0)
        right_open = jnp.where(me < parts - 1, rigid_ref[0], 0.0)
        edge = jnp.concatenate(
            [
                left_open * (own[slots : slots + 1] - before[slots + 1 : slots + 2]),
                right_open * (own[slots + 1 : slots + 2] - after[slots : slots + 1]),
                jnp.zeros((6, width), jnp.float32),
            ],
            axis=0,
        )
        force_ref[parts * slots : parts * slots + 8, :] = edge
        return split_three(force_ref[...] * scale)

    send_anchors(0, value_ref)

    lane = lax.broadcasted_iota(jnp.int32, (1, width), 1)
    rigid = rigid_ref[0]
    cuts = []
    running = nodes_ref[0, 0]
    for j in range(1, nodes_ref.shape[1]):
        cuts.append(running)
        running = running + nodes_ref[0, j]
    cuts.append(running)
    for r in range(count // width):
        place = lane + r * width
        open_link = place < CABLE_ROWS - 1
        for cut in cuts:
            open_link = open_link & (place + 1 != cut)
        deck_link = (place >= CABLE_ROWS) & (place < count - 1)
        link = jnp.where(open_link, stiff_ref[r : r + 1, :], jnp.where(deck_link, rigid, 0.0))
        lo = PAD + r * width
        link_ref[lo : lo + width, :] = jnp.broadcast_to(link, (width, width)).T
        mass = mass_ref[r : r + 1, :] - center
        diag_ref[r * width : (r + 1) * width, :] = jnp.broadcast_to(mass, (width, width)).T

    def base(ref, lo):
        at = PAD + lo
        here = ref[at : at + chunk, :]
        down = link_ref[at : at + chunk, :] * (here - ref[at + 1 : at + chunk + 1, :])
        up = link_ref[at - 1 : at + chunk - 1, :] * (here - ref[at - 1 : at + chunk - 1, :])
        return diag_ref[lo : lo + chunk, :] * here + down + up

    for lo in range(0, count, chunk):
        first_ref[PAD + lo : PAD + lo + chunk, :] = base(value_ref, lo) * inverse_half
        node = lax.broadcasted_iota(jnp.int32, (chunk, target_ref.shape[1]), 0) + lo
        hot_ref[lo : lo + chunk, :] = jnp.where(node == target_ref[...], 1.0, 0.0).astype(jnp.bfloat16)

    pulls = collect(0, inverse_half)
    for lo in range(0, count, chunk):
        first_ref[PAD + lo : PAD + lo + chunk, :] += jnp.dot(
            hot_ref[lo : lo + chunk, :], pulls, preferred_element_type=jnp.float32
        )
    send_anchors(1, first_ref)
    double = 2.0 * inverse_half
    for lo in range(0, count, chunk):
        diag_ref[lo : lo + chunk, :] = (
            base(first_ref, lo) * double - value_ref[PAD + lo : PAD + lo + chunk, :]
        )
    pulls = collect(1, double)
    for lo in range(0, count, chunk):
        cols_ref[col, lo : lo + chunk, :] = (
            diag_ref[lo : lo + chunk, :]
            + jnp.dot(hot_ref[lo : lo + chunk, :], pulls, preferred_element_type=jnp.float32)
        ).astype(jnp.bfloat16)

    def share(owner, target, piece, k, i):
        rows = pl.ds(pl.multiple_of(piece * chunk, chunk), chunk)
        return pltpu.make_async_remote_copy(
            src_ref=cols_ref.at[owner, rows],
            dst_ref=cols_ref.at[owner, rows],
            send_sem=quarter_send.at[k, i],
            recv_sem=quarter_recv.at[k, i],
            device_id=(me, target),
            device_id_type=MESH,
        )

    for k in range(1, splits):
        target = lax.rem(col + k, splits)
        share(col, target, target, k, 0).start()
    for k in range(1, splits):
        share(lax.rem(col + splits - k, splits), col, col, k, 0).wait_recv()

    mine = pl.ds(pl.multiple_of(col * chunk, chunk), chunk)
    packed = jnp.concatenate([cols_ref[b, mine, :] for b in range(splits)], axis=1)
    for i in range(splits):
        rows = lax.dot_general(
            packed[:, i * width : (i + 1) * width],
            packed[:, : (i + 1) * width],
            (((0,), (0,)), ((), ())),
            preferred_element_type=jnp.float32,
        )
        for j in range(i + 1):
            at = (i * (i + 1) // 2 + j) * width
            sum_ref[at : at + width, :] = rows[:, j * width : (j + 1) * width]
    length = sum_ref.shape[0]
    used = splits * (splits + 1) // 2 * width
    if used < length:
        sum_ref[used:, :] = jnp.zeros((length - used, width), jnp.float32)

    bits = splits.bit_length() - 1
    start = 0
    offset = 0
    for b in range(bits):
        half = length >> (b + 1)
        bit = lax.rem(col // (1 << b), 2)
        partner = col + (1 << b) * (1 - 2 * bit)
        landing = half_ref.at[pl.ds(offset, half)]
        copy = pltpu.make_async_remote_copy(
            src_ref=sum_ref.at[pl.ds(pl.multiple_of(start + (1 - bit) * half, 8), half)],
            dst_ref=landing,
            send_sem=fold_send.at[b],
            recv_sem=fold_recv.at[b],
            device_id=(me, partner),
            device_id_type=MESH,
        )
        copy.start()
        copy.wait()
        start = pl.multiple_of(start + bit * half, 8)
        sum_ref[pl.ds(start, half), :] += half_ref[offset : offset + half, :]
        offset += half
    part = length // splits
    unit = part // parts

    def piece(q):
        return pl.ds(pl.multiple_of(start + q * unit, 8), unit)

    def send_piece(k, carry):
        target = lax.rem(me + k, parts)
        pltpu.make_async_remote_copy(
            src_ref=sum_ref.at[piece(target)],
            dst_ref=piece_ref.at[me],
            send_sem=piece_send.at[k],
            recv_sem=piece_recv.at[k],
            device_id=(target, col),
            device_id_type=MESH,
        ).start()
        return carry

    def piece_copy(k):
        source = lax.rem(me + parts - k, parts)
        return pltpu.make_async_remote_copy(
            src_ref=sum_ref.at[piece(source)],
            dst_ref=piece_ref.at[source],
            send_sem=piece_send.at[k],
            recv_sem=piece_recv.at[k],
            device_id=(source, col),
            device_id_type=MESH,
        )

    lax.fori_loop(1, parts, send_piece, 0, unroll=unroll)

    def add_piece(k, total):
        piece_copy(k).wait_recv()
        return total + piece_ref[lax.rem(me + parts - k, parts)]

    all_ref[piece(me), :] = lax.fori_loop(1, parts, add_piece, sum_ref[piece(me), :], unroll=unroll)

    def give(owner, target, k):
        return pltpu.make_async_remote_copy(
            src_ref=all_ref.at[piece(owner)],
            dst_ref=all_ref.at[piece(owner)],
            send_sem=give_send.at[k],
            recv_sem=give_recv.at[k],
            device_id=(target, col),
            device_id_type=MESH,
        )

    def give_start(k, carry):
        give(me, lax.rem(me + k, parts), k).start()
        return carry

    def give_wait(k, carry):
        give(lax.rem(me + parts - k, parts), me, k).wait_recv()
        return carry

    lax.fori_loop(1, parts, give_start, 0, unroll=unroll)
    lax.fori_loop(1, parts, give_wait, 0, unroll=unroll)
    grown = []
    held = part
    for b in reversed(range(bits)):
        bit = lax.rem(col // (1 << b), 2)
        partner = col + (1 << b) * (1 - 2 * bit)

        def grow(at):
            rows = pl.ds(pl.multiple_of(at, 8), held)
            return pltpu.make_async_remote_copy(
                src_ref=all_ref.at[rows],
                dst_ref=all_ref.at[rows],
                send_sem=grow_send.at[b],
                recv_sem=grow_recv.at[b],
                device_id=(me, partner),
                device_id_type=MESH,
            )

        copy = grow(start)
        copy.start()
        grown.append(copy)
        grow(start + (1 - 2 * bit) * held).wait_recv()
        start = start - bit * held
        held = 2 * held

    for k in range(1, splits):
        target = lax.rem(col + k, splits)
        for i in range(1, splits):
            share(col, target, lax.rem(target + i, splits), k, i).start()

    for i in range(splits):
        for j in range(i + 1):
            at = (i * (i + 1) // 2 + j) * width
            gram_ref[i * width : (i + 1) * width, j * width : (j + 1) * width] = all_ref[
                at : at + width, :
            ] * (1.0 / total_rows)
    inverse_factor(gram_ref, inv_ref)

    for k in range(1, splits):
        for i in range(1, splits):
            share(lax.rem(col + splits - k, splits), col, lax.rem(col + i, splits), k, i).wait_recv()
    factor = inv_ref[pl.ds(pl.multiple_of(col * width, width), width), :].astype(jnp.bfloat16)
    for lo in range(0, count, chunk):
        block = jnp.concatenate([cols_ref[b, lo : lo + chunk, :] for b in range(splits)], axis=1)
        out_ref[lo : lo + chunk, :] = lax.dot_general(
            block, factor, (((1,), (1,)), ((), ())), preferred_element_type=jnp.float32
        ).astype(jnp.bfloat16)

    for k in range(1, splits):
        target = lax.rem(col + k, splits)
        for i in range(splits):
            share(col, target, lax.rem(target + i, splits), k, i).wait_send()
    for copy in grown:
        copy.wait_send()

    def settle(k, carry):
        target = lax.rem(me + k, parts)
        remote(0, k, target).wait_send()
        remote(1, k, target).wait_send()
        piece_copy(k).wait_send()
        give(me, target, k).wait_send()
        return carry

    lax.fori_loop(1, parts, settle, 0, unroll=unroll)


def body(
    parts,
    splits,
    vectors,
    node_mass,
    cable_stiff,
    cable_nodes,
    deck_rigidity,
    anchor_rows,
    anchor_stiff,
    cut_low,
    top_bound,
):
    count, width = vectors.shape
    slots = anchor_rows.shape[2]
    places = jnp.concatenate(
        [
            anchor_rows.reshape(1, -1),
            jnp.array([[CABLE_ROWS, count - 1] + [count] * 6], jnp.int32),
        ],
        axis=1,
    )
    targets = jnp.tile(places, (1, 3))
    size = splits * width
    blocks = splits * (splits + 1) // 2
    unit = -(-(blocks * width) // (splits * parts * 8)) * 8
    length = unit * parts * splits
    bits = splits.bit_length() - 1
    vmem = pl.BlockSpec(memory_space=pltpu.VMEM)
    smem = pl.BlockSpec(memory_space=pltpu.SMEM)
    sem = pltpu.SemaphoreType.DMA
    f32 = jnp.float32
    return pl.pallas_call(
        functools.partial(kernel, parts, splits),
        out_shape=jax.ShapeDtypeStruct((count, width), jnp.bfloat16),
        in_specs=[vmem, vmem, vmem, smem, smem, smem, smem, smem, smem, vmem],
        out_specs=vmem,
        scratch_shapes=[
            pltpu.VMEM((count + 2 * PAD, width), f32),
            pltpu.VMEM((count + 2 * PAD, width), f32),
            pltpu.VMEM((count + 2 * PAD, width), f32),
            pltpu.VMEM((count, width), f32),
            pltpu.VMEM((count, targets.shape[1]), jnp.bfloat16),
            pltpu.VMEM((places.shape[1], width), f32),
            pltpu.VMEM((2, parts, 8, width), f32),
            pltpu.VMEM((2, parts, 8, width), f32),
            pltpu.VMEM((splits, count, width), jnp.bfloat16),
            pltpu.VMEM((length, width), f32),
            pltpu.VMEM((length, width), f32),
            pltpu.VMEM((parts, unit, width), f32),
            pltpu.VMEM((length, width), f32),
            pltpu.VMEM((size, size), f32),
            pltpu.VMEM((size, size), f32),
            sem((2, parts)),
            sem((2, parts)),
            sem((splits, splits)),
            sem((splits, splits)),
            sem((bits,)),
            sem((bits,)),
            sem((parts,)),
            sem((parts,)),
            sem((parts,)),
            sem((parts,)),
            sem((bits,)),
            sem((bits,)),
        ],
        compiler_params=pltpu.CompilerParams(
            collective_id=0, has_side_effects=True, vmem_limit_bytes=60 * 1024 * 1024
        ),
    )(
        vectors,
        node_mass.reshape(-1, width),
        cable_stiff.reshape(-1, width),
        cable_nodes,
        deck_rigidity.reshape(1),
        anchor_rows.reshape(-1, slots),
        anchor_stiff.reshape(-1, slots),
        cut_low.reshape(1),
        top_bound.reshape(1),
        targets,
    )


def solution(mesh):
    return jax.shard_map(
        functools.partial(body, mesh.shape["rows"], mesh.shape["vecs"]),
        mesh=mesh,
        in_specs=(
            P("rows", "vecs"),
            P("rows"),
            P("rows"),
            P("rows", None),
            P(),
            P("rows", None, None),
            P("rows", None, None),
            P(),
            P(),
        ),
        out_specs=P("rows", "vecs"),
        check_vma=False,
    )
```

time: 261 us -> 128 us (0.49)
  waiting for transfers between devices: 111 us -> 0 us
  Pallas kernels: 72.5 us -> 119 us
  other arithmetic: 27.2 us -> 0.07 us
  starting transfers between devices: 21.8 us -> 0 us
  between operations: 15.6 us -> 1.97 us
  matrix products: 8.43 us -> 0 us
  local copies, waits for them, and re-layouts: 2.75 us -> 5.49 us
    psum x1 -> x0, waiting for transfers between devices: 79.1 us -> none  [body(): gram_matrix = lax.psum(gram_whole, 'rows') / total_rows]
    pallas_call x1, Pallas kernels: 72.5 us -> 119 us  [body(): pl.pallas_call(functools.partial(kernel, parts, splits), out_shape=jax.Sh...]
    all_gather x1 -> x0, waiting for transfers between devices: 29.7 us -> none  [body(): columns = lax.all_gather(filtered, 'vecs', axis=1, tiled=True)]
    all_to_all x2 -> x0, starting transfers between devices: 12.5 us -> none  [apply_operator(): lax.all_to_all(outgoing.astype(jnp.bfloat16), 'rows', split_axis=0, conca...]
    ppermute x4 -> x0, starting transfers between devices: 9.07 us -> none  [the longest x2 6.48 us: with_halo(): lax.ppermute(lax.slice_in_dim(block, block.shape[dim] - width, None, axis...]
    dot_general x2 -> x0, matrix products: 8.43 us -> none  [the longest x1 5.62 us: body(): jnp.einsum('rb,rc->bc', columns, columns, preferred_element_type=jnp.floa...]
    scatter-add x2 -> x0, other arithmetic: 6.51 us -> none  [apply_operator(): jnp.zeros_like(values).at[flat_rows].add(anchor_force, mode='drop')]
    convert_element_type x4 -> x0, other arithmetic: 5.25 us -> none  [the longest x1 2.64 us: body(): filtered = second_degree.astype(jnp.bfloat16)]
  transfers between devices with their start and end apart: 8 -> 0, of which waited for: 3 -> 0; matrix products, arithmetic and copies ran while one was open for 5% -> 0% of each run, Pallas kernels for 0% -> 0%
where the time goes in v2:
time: 128 us; the launch traced here: 126 us
  Pallas kernels  119 us (93%)
  local copies, waits for them, and re-layouts  5.49 us (4%)
  between operations  1.97 us (2%)
    pallas_call x1, Pallas kernels, body(): pl.pallas_call(functools.partial(kernel, parts, splits), out_shape=jax.Sh...  119 us
    unnamed x8, local copies, waits for them, and re-layouts  3.41 us

profile of v2, /device:TPU:3, one launch (start us, length us, event | category | flops | bytes accessed | tf_op | source)
XLA Modules:
  0.0 126.5 jit_solution(15963428817207833064)
XLA Ops:
  1.9 0.0 copy-start.1
  2.0 0.7 copy-done.1
  2.6 0.0 copy-start
  2.6 0.7 copy.16.spring_ref
  3.3 0.0 copy-done
  3.3 0.7 copy.15.rows_ref
  4.0 0.1 copy.14
  4.1 0.0 copy-start.2
  4.1 0.1 reshape.37
  4.1 0.6 copy-done.2
  4.7 0.1 add_bitcast_fusion
  4.8 0.7 tile.13.target_ref
  5.5 119.0 %shard_map.100 = bf16[3072,128]{1,0:T(8,128)(2,1)} custom-call(bf16[3072,128]{1,0:T(8,128)(2,1)} %x_ref.1, f32[24,128]{1,0:T(8,128)} %bitcast.12, f32[24,128]{1,0:T(8,128)} %bitcast.13, s32[1,4]{1,0:T(1,128)} %nodes_ref.1, f32[1]{0:T(128)} %bitcast.9.rigid_ref, s32[8,4]{1,0:T(8,128)} %copy.15.rows_ref, f32[8,4]{1,0:T(8,128)} %copy.16.spring_ref, ...), custom_call_target="tpu_custom_call" | custom-call | tf_op jit(solution)/shard_map/pallas_call | solution.py:487
  124.4 2.1 %copy.21 = bf16[3072,128]{1,0:T(8,128)(2,1)} copy(bf16[3072,128]{1,0:T(8,128)(2,1)} %shard_map.100) | data formatting | bytes 1572864
  (1 shorter events, 0.0 us)
Async XLA Ops:
  1.9 0.7 copy-start.1
  2.6 0.7 copy-start
  4.1 0.7 copy-start.2

commit v3 on v2

--- a/solution.py
+++ b/solution.py
@@ -11,8 +11,13 @@
 MESH = pl.DeviceIdType.MESH
 PAD = 8
 
+
 NB = 128
 HI = lax.Precision.HIGHEST
+
+
+def spread(tile, lane):
+    return jnp.broadcast_to(tile[:, lane : lane + 1], tile.shape)
 
 
 def eliminate(block):
@@ -21,25 +26,32 @@
     tiles = NB // 8
     left = [block[8 * t : 8 * t + 8, :] for t in range(tiles)]
     right = [jnp.where(lane == sub + 8 * t, 1.0, 0.0).astype(jnp.float32) for t in range(tiles)]
-    for j in range(NB):
-        home, row = divmod(j, 8)
-        pivot_row = left[home][row : row + 1, :]
-        scale = lax.rsqrt(pivot_row[:, j : j + 1])
-        scaled = pivot_row * scale
-        inverse_row = right[home][row : row + 1, :] * scale
-        scaled_all = jnp.broadcast_to(scaled, (8, NB))
-        inverse_all = jnp.broadcast_to(inverse_row, (8, NB))
-        for t in range(home, tiles):
-            column = jnp.broadcast_to(left[t][:, j : j + 1], (8, NB)) * scale
-            if t == home:
-                below = sub > row
-                left[t] = jnp.where(below, left[t] - column * scaled_all, left[t])
-                right[t] = jnp.where(
-                    below, right[t] - column * inverse_all, jnp.where(sub == row, inverse_all, right[t])
-                )
-            else:
-                left[t] = left[t] - column * scaled_all
-                right[t] = right[t] - column * inverse_all
+    for g in range(tiles):
+        home, away = left[g], right[g]
+        column = [spread(home, 8 * g + i) for i in range(8)]
+        scales, rows = [], []
+        for i in range(8):
+            scale = lax.rsqrt(column[i][i : i + 1, :])
+            scales.append(scale)
+            column[i] = column[i] * scale
+            rows.append([column[i][n : n + 1, :] for n in range(8)])
+            for n in range(i + 1, 8):
+                column[n] = column[n] - column[i] * rows[i][n]
+        for i in range(8):
+            upper = home[i : i + 1, :] * scales[i]
+            inverse = away[i : i + 1, :] * scales[i]
+            home = jnp.where(sub > i, home - column[i] * upper, jnp.where(sub == i, upper, home))
+            away = jnp.where(sub > i, away - column[i] * inverse, jnp.where(sub == i, inverse, away))
+        right[g] = away
+        for t in range(g + 1, tiles):
+            factor = [spread(left[t], 8 * g + i) for i in range(8)]
+            for i in range(8):
+                factor[i] = factor[i] * scales[i]
+                for n in range(i + 1, 8):
+                    factor[n] = factor[n] - factor[i] * rows[i][n]
+            for i in range(8):
+                left[t] = left[t] - factor[i] * home[i : i + 1, :]
+                right[t] = right[t] - factor[i] * away[i : i + 1, :]
     return jnp.concatenate(right, axis=0)
 
 
@@ -47,12 +59,14 @@
     return lax.dot_general(a, b, (dims, ((), ())), precision=HI, preferred_element_type=jnp.float32)
 
 
-def inverse_factor(gram_ref, inv_ref):
+def inverse_factor(gram_ref, inv_ref, between):
     size = gram_ref.shape[0]
     inv_ref[...] = jnp.zeros_like(inv_ref)
     for k in range(size // NB):
         lo, hi = k * NB, (k + 1) * NB
         diag_inv = eliminate(gram_ref[lo:hi, lo:hi])
+        if k == (size // NB - 1) // 2:
+            between()
         if k:
             inv_ref[lo:hi, :lo] = mm(diag_inv, inv_ref[lo:hi, :lo], ((1,), (0,)))
         inv_ref[lo:hi, lo:hi] = diag_inv
@@ -62,6 +76,23 @@
                 part = panel[i - hi : i - hi + NB]
                 gram_ref[i : i + NB, hi : i + NB] -= mm(part, panel[: i - hi + NB], ((1,), (1,)))
             inv_ref[hi:, :hi] -= mm(panel, inv_ref[lo:hi, :hi], ((1,), (0,)))
+
+
+def travel_plan(splits):
+    if splits != 4:
+        direct = [
+            (block, target, block, piece)
+            for target in range(splits)
+            for block in range(target)
+            for piece in range(splits)
+            if piece != target
+        ]
+        return direct, []
+    first = [(0, 2, 0, 0), (0, 3, 0, 1), (1, 2, 1, 0), (1, 3, 1, 1)]
+    first += [(2, 3, 0, 2), (2, 3, 1, 2), (3, 2, 0, 3), (3, 2, 1, 3)]
+    first += [(0, 1, 0, 0), (0, 1, 0, 2), (0, 1, 0, 3), (2, 3, 2, 0), (2, 3, 2, 1), (2, 3, 2, 2)]
+    second = [(2, 3, 0, 0), (2, 3, 1, 0), (3, 2, 0, 1), (3, 2, 1, 1)]
+    return first, second
 
 
 def split_three(value):
@@ -84,7 +115,6 @@
     spring_ref,
     low_ref,
     top_ref,
-    target_ref,
     out_ref,
     value_ref,
     first_ref,
@@ -105,6 +135,8 @@
     ex_recv,
     quarter_send,
     quarter_recv,
+    travel_send,
+    travel_recv,
     fold_send,
     fold_recv,
     piece_send,
@@ -117,7 +149,7 @@
     me = lax.axis_index("rows")
     col = lax.axis_index("vecs")
     count, width = x_ref.shape
-    slots = rows_ref.shape[1]
+    slots = rows_ref.shape[2]
     total_rows = count * parts
 
     barrier = pltpu.get_barrier_semaphore()
@@ -178,7 +210,7 @@
 
         def pick(q, carry):
             picked = [
-                ref[pl.ds(PAD + jnp.minimum(rows_ref[q, s], count - 1), 1), :] for s in range(slots)
+                ref[pl.ds(PAD + jnp.minimum(rows_ref[0, q, s], count - 1), 1), :] for s in range(slots)
             ]
             send_buf[turn, q] = jnp.concatenate(picked + [first_row, last_row, blank], axis=0)
             return carry
@@ -202,7 +234,7 @@
         def pull(q, carry):
             difference = send_buf[turn, q] - recv_buf[turn, q]
             for s in range(slots):
-                live = jnp.where(rows_ref[q, s] < count, spring_ref[q, s], 0.0)
+                live = jnp.where(rows_ref[0, q, s] < count, spring_ref[0, q, s], 0.0)
                 force_ref[pl.ds(q * slots + s, 1), :] = live * difference[s : s + 1, :]
             return carry
 
@@ -224,6 +256,18 @@
         return split_three(force_ref[...] * scale)
 
     send_anchors(0, value_ref)
+
+    forces = force_ref.shape[0]
+    order = lax.rem(lax.broadcasted_iota(jnp.int32, (1, 3 * forces), 1), forces)
+    ends = parts * slots
+    target = jnp.where(order == ends, CABLE_ROWS, jnp.where(order == ends + 1, count - 1, count))
+
+    def place_anchor(q, carry):
+        for s in range(slots):
+            carry = jnp.where(order == q * slots + s, rows_ref[0, q, s], carry)
+        return carry
+
+    target = lax.fori_loop(0, parts, place_anchor, target, unroll=unroll)
 
     lane = lax.broadcasted_iota(jnp.int32, (1, width), 1)
     rigid = rigid_ref[0]
@@ -254,8 +298,8 @@
 
     for lo in range(0, count, chunk):
         first_ref[PAD + lo : PAD + lo + chunk, :] = base(value_ref, lo) * inverse_half
-        node = lax.broadcasted_iota(jnp.int32, (chunk, target_ref.shape[1]), 0) + lo
-        hot_ref[lo : lo + chunk, :] = jnp.where(node == target_ref[...], 1.0, 0.0).astype(jnp.bfloat16)
+        node = lax.broadcasted_iota(jnp.int32, (chunk, 3 * forces), 0) + lo
+        hot_ref[lo : lo + chunk, :] = jnp.where(node == target, 1.0, 0.0).astype(jnp.bfloat16)
 
     pulls = collect(0, inverse_half)
     for lo in range(0, count, chunk):
@@ -275,22 +319,22 @@
             + jnp.dot(hot_ref[lo : lo + chunk, :], pulls, preferred_element_type=jnp.float32)
         ).astype(jnp.bfloat16)
 
-    def share(owner, target, piece, k, i):
+    def share(owner, target, piece, k):
         rows = pl.ds(pl.multiple_of(piece * chunk, chunk), chunk)
         return pltpu.make_async_remote_copy(
             src_ref=cols_ref.at[owner, rows],
             dst_ref=cols_ref.at[owner, rows],
-            send_sem=quarter_send.at[k, i],
-            recv_sem=quarter_recv.at[k, i],
+            send_sem=quarter_send.at[k],
+            recv_sem=quarter_recv.at[k],
             device_id=(me, target),
             device_id_type=MESH,
         )
 
     for k in range(1, splits):
         target = lax.rem(col + k, splits)
-        share(col, target, target, k, 0).start()
+        share(col, target, target, k).start()
     for k in range(1, splits):
-        share(lax.rem(col + splits - k, splits), col, col, k, 0).wait_recv()
+        share(lax.rem(col + splits - k, splits), col, col, k).wait_recv()
 
     mine = pl.ds(pl.multiple_of(col * chunk, chunk), chunk)
     packed = jnp.concatenate([cols_ref[b, mine, :] for b in range(splits)], axis=1)
@@ -411,10 +455,38 @@
         start = start - bit * held
         held = 2 * held
 
-    for k in range(1, splits):
-        target = lax.rem(col + k, splits)
-        for i in range(1, splits):
-            share(col, target, lax.rem(target + i, splits), k, i).start()
+    first_trips, second_trips = travel_plan(splits)
+
+    def trip(number):
+        _, target, block, piece = (first_trips + second_trips)[number]
+        rows = pl.ds(piece * chunk, chunk)
+        return pltpu.make_async_remote_copy(
+            src_ref=cols_ref.at[block, rows],
+            dst_ref=cols_ref.at[block, rows],
+            send_sem=travel_send.at[number],
+            recv_sem=travel_recv.at[number],
+            device_id=(me, target),
+            device_id_type=MESH,
+        )
+
+    def each_trip(numbers, end, act):
+        trips = first_trips + second_trips
+        for device in range(splits):
+            own = [n for n in numbers if trips[n][end] == device]
+            if own:
+
+                @pl.when(col == device)
+                def _():
+                    for n in own:
+                        act(trip(n))
+
+    early = range(len(first_trips))
+    late = range(len(first_trips), len(first_trips) + len(second_trips))
+    each_trip(early, 0, lambda copy: copy.start())
+
+    def pass_on():
+        each_trip(early, 1, lambda copy: copy.wait_recv())
+        each_trip(late, 0, lambda copy: copy.start())
 
     for i in range(splits):
         for j in range(i + 1):
@@ -422,22 +494,27 @@
             gram_ref[i * width : (i + 1) * width, j * width : (j + 1) * width] = all_ref[
                 at : at + width, :
             ] * (1.0 / total_rows)
-    inverse_factor(gram_ref, inv_ref)
-
-    for k in range(1, splits):
-        for i in range(1, splits):
-            share(lax.rem(col + splits - k, splits), col, lax.rem(col + i, splits), k, i).wait_recv()
-    factor = inv_ref[pl.ds(pl.multiple_of(col * width, width), width), :].astype(jnp.bfloat16)
-    for lo in range(0, count, chunk):
-        block = jnp.concatenate([cols_ref[b, lo : lo + chunk, :] for b in range(splits)], axis=1)
-        out_ref[lo : lo + chunk, :] = lax.dot_general(
-            block, factor, (((1,), (1,)), ((), ())), preferred_element_type=jnp.float32
-        ).astype(jnp.bfloat16)
+    inverse_factor(gram_ref, inv_ref, pass_on)
+    each_trip(late, 1, lambda copy: copy.wait_recv())
+
+    for device in range(splits):
+
+        @pl.when(col == device)
+        def _():
+            used_width = (device + 1) * width
+            factor = inv_ref[device * width : used_width, :used_width].astype(jnp.bfloat16)
+            for lo in range(0, count, chunk):
+                block = jnp.concatenate(
+                    [cols_ref[b, lo : lo + chunk, :] for b in range(device + 1)], axis=1
+                )
+                out_ref[lo : lo + chunk, :] = lax.dot_general(
+                    block, factor, (((1,), (1,)), ((), ())), preferred_element_type=jnp.float32
+                ).astype(jnp.bfloat16)
 
     for k in range(1, splits):
         target = lax.rem(col + k, splits)
-        for i in range(splits):
-            share(col, target, lax.rem(target + i, splits), k, i).wait_send()
+        share(col, target, target, k).wait_send()
+    each_trip(range(len(first_trips) + len(second_trips)), 0, lambda copy: copy.wait_send())
     for copy in grown:
         copy.wait_send()
 
@@ -467,14 +544,8 @@
 ):
     count, width = vectors.shape
     slots = anchor_rows.shape[2]
-    places = jnp.concatenate(
-        [
-            anchor_rows.reshape(1, -1),
-            jnp.array([[CABLE_ROWS, count - 1] + [count] * 6], jnp.int32),
-        ],
-        axis=1,
-    )
-    targets = jnp.tile(places, (1, 3))
+    forces = parts * slots + 8
+    trips = sum(len(trips) for trips in travel_plan(splits))
     size = splits * width
     blocks = splits * (splits + 1) // 2
     unit = -(-(blocks * width) // (splits * parts * 8)) * 8
@@ -487,15 +558,15 @@
     return pl.pallas_call(
         functools.partial(kernel, parts, splits),
         out_shape=jax.ShapeDtypeStruct((count, width), jnp.bfloat16),
-        in_specs=[vmem, vmem, vmem, smem, smem, smem, smem, smem, smem, vmem],
+        in_specs=[vmem, vmem, vmem, smem, smem, smem, smem, smem, smem],
         out_specs=vmem,
         scratch_shapes=[
             pltpu.VMEM((count + 2 * PAD, width), f32),
             pltpu.VMEM((count + 2 * PAD, width), f32),
             pltpu.VMEM((count + 2 * PAD, width), f32),
             pltpu.VMEM((count, width), f32),
-            pltpu.VMEM((count, targets.shape[1]), jnp.bfloat16),
-            pltpu.VMEM((places.shape[1], width), f32),
+            pltpu.VMEM((count, 3 * forces), jnp.bfloat16),
+            pltpu.VMEM((forces, width), f32),
             pltpu.VMEM((2, parts, 8, width), f32),
             pltpu.VMEM((2, parts, 8, width), f32),
             pltpu.VMEM((splits, count, width), jnp.bfloat16),
@@ -507,8 +578,10 @@
             pltpu.VMEM((size, size), f32),
             sem((2, parts)),
             sem((2, parts)),
-            sem((splits, splits)),
-            sem((splits, splits)),
+            sem((splits,)),
+            sem((splits,)),
+            sem((trips,)),
+            sem((trips,)),
             sem((bits,)),
             sem((bits,)),
             sem((parts,)),
@@ -527,11 +600,10 @@
         cable_stiff.reshape(-1, width),
         cable_nodes,
         deck_rigidity.reshape(1),
-        anchor_rows.reshape(-1, slots),
-        anchor_stiff.reshape(-1, slots),
+        anchor_rows,
+        anchor_stiff,
         cut_low.reshape(1),
         top_bound.reshape(1),
-        targets,
     )
 
 

time: 128 us -> 73.8 us (0.58)
  Pallas kernels: 119 us -> 67.5 us
  local copies, waits for them, and re-layouts: 5.49 us -> 4.09 us
    pallas_call x1, Pallas kernels: 119 us -> 67.5 us  [body(): pl.pallas_call(functools.partial(kernel, parts, splits), out_shape=jax.Sh...]
    reshape x3 -> x0, local copies, waits for them, and re-layouts: 1.41 us -> none  [the longest x1 0.67 us: body(): anchor_rows.reshape(-1, slots)]
    unnamed x8 -> x7, local copies, waits for them, and re-layouts: 3.41 us -> 4.09 us
where the time goes in v3:
time: 73.8 us; the launch traced here: 73.6 us
  Pallas kernels  67.5 us (91%)
  local copies, waits for them, and re-layouts  4.09 us (6%)
  between operations  1.96 us (3%)
    pallas_call x1, Pallas kernels, body(): pl.pallas_call(functools.partial(kernel, parts, splits), out_shape=jax.Sh...  67.5 us
    unnamed x7, local copies, waits for them, and re-layouts  4.09 us

profile of v3, /device:TPU:3, one launch (start us, length us, event | category | flops | bytes accessed | tf_op | source)
XLA Modules:
  0.0 73.6 jit_solution(11030444788787831583)
XLA Ops:
  1.9 0.0 copy-start
  2.0 0.7 copy-done
  2.6 0.0 copy-start.1
  2.6 0.7 copy.10.rows_ref
  3.3 0.0 copy-done.1
  3.3 0.7 copy.11.spring_ref
  4.0 67.5 %shard_map.91 = bf16[3072,128]{1,0:T(8,128)(2,1)} custom-call(bf16[3072,128]{1,0:T(8,128)(2,1)} %x_ref.1, f32[24,128]{1,0:T(8,128)} %bitcast.8, f32[24,128]{1,0:T(8,128)} %bitcast.9, s32[1,4]{1,0:T(1,128)} %nodes_ref.1, f32[1]{0:T(128)} %bitcast.5.rigid_ref, s32[1,8,4]{2,1,0:T(8,128)} %copy.10.rows_ref, f32[1,8,4]{2,1,0:T(8,128)} %copy.11.spring_ref, ...), custom_call_target="tpu_custom_call" | custom-call | tf_op jit(solution)/shard_map/pallas_call | solution.py:558
  71.5 2.1 %copy.16 = bf16[3072,128]{1,0:T(8,128)(2,1)} copy(bf16[3072,128]{1,0:T(8,128)(2,1)} %shard_map.91) | data formatting | bytes 1572864
Async XLA Ops:
  1.9 0.7 copy-start
  2.6 0.7 copy-start.1

commit v4 on v3

--- a/solution.py
+++ b/solution.py
@@ -145,6 +145,8 @@
     give_recv,
     grow_send,
     grow_recv,
+    relay_send,
+    relay_recv,
 ):
     me = lax.axis_index("rows")
     col = lax.axis_index("vecs")
@@ -430,10 +432,44 @@
         return carry
 
     lax.fori_loop(1, parts, give_start, 0, unroll=unroll)
-    lax.fori_loop(1, parts, give_wait, 0, unroll=unroll)
+    last_bit = lax.rem(col // (splits // 2), 2)
+    last_partner = col + (splits // 2) * (1 - 2 * last_bit)
+    across = start + (1 - 2 * last_bit) * part
+
+    def relay(region, k):
+        source = lax.rem(me + parts - k, parts)
+        rows = pl.ds(pl.multiple_of(region + source * unit, 8), unit)
+        return pltpu.make_async_remote_copy(
+            src_ref=all_ref.at[rows],
+            dst_ref=all_ref.at[rows],
+            send_sem=relay_send.at[k],
+            recv_sem=relay_recv.at[k],
+            device_id=(me, last_partner),
+            device_id_type=MESH,
+        )
+
+    relay(start, 0).start()
+
+    def relay_start(k, carry):
+        give_wait(k, carry)
+        relay(start, k).start()
+        return carry
+
+    def relay_wait(k, carry):
+        relay(across, k).wait_recv()
+        return carry
+
+    lax.fori_loop(1, parts, relay_start, 0, unroll=unroll)
+    lax.fori_loop(0, parts, relay_wait, 0, unroll=unroll)
+
+    def relay_end(k, carry):
+        relay(across, k).wait_send()
+        return carry
+
+    start = start - last_bit * part
     grown = []
-    held = part
-    for b in reversed(range(bits)):
+    held = 2 * part
+    for b in reversed(range(bits - 1)):
         bit = lax.rem(col // (1 << b), 2)
         partner = col + (1 << b) * (1 - 2 * bit)
 
@@ -527,6 +563,7 @@
         return carry
 
     lax.fori_loop(1, parts, settle, 0, unroll=unroll)
+    lax.fori_loop(0, parts, relay_end, 0, unroll=unroll)
 
 
 def body(
@@ -590,6 +627,8 @@
             sem((parts,)),
             sem((bits,)),
             sem((bits,)),
+            sem((parts,)),
+            sem((parts,)),
         ],
         compiler_params=pltpu.CompilerParams(
             collective_id=0, has_side_effects=True, vmem_limit_bytes=60 * 1024 * 1024

time: 73.8 us -> 73.7 us (level)
  no operation moved by 1% of the time
where the time goes in v4:
time: 73.7 us; the launch traced here: 73.5 us
  Pallas kernels  67.4 us (91%)
  local copies, waits for them, and re-layouts  4.09 us (6%)
  between operations  1.96 us (3%)
    pallas_call x1, Pallas kernels, body(): pl.pallas_call(functools.partial(kernel, parts, splits), out_shape=jax.Sh...  67.4 us
    unnamed x7, local copies, waits for them, and re-layouts  4.09 us

profile of v4, /device:TPU:3, one launch (start us, length us, event | category | flops | bytes accessed | tf_op | source)
XLA Modules:
  0.0 73.5 jit_solution(15417834437949198523)
XLA Ops:
  1.9 0.0 copy-start
  2.0 0.7 copy-done
  2.6 0.0 copy-start.1
  2.6 0.7 copy.10.rows_ref
  3.3 0.0 copy-done.1
  3.3 0.7 copy.11.spring_ref
  4.0 67.4 %shard_map.91 = bf16[3072,128]{1,0:T(8,128)(2,1)} custom-call(bf16[3072,128]{1,0:T(8,128)(2,1)} %x_ref.1, f32[24,128]{1,0:T(8,128)} %bitcast.8, f32[24,128]{1,0:T(8,128)} %bitcast.9, s32[1,4]{1,0:T(1,128)} %nodes_ref.1, f32[1]{0:T(128)} %bitcast.5.rigid_ref, s32[1,8,4]{2,1,0:T(8,128)} %copy.10.rows_ref, f32[1,8,4]{2,1,0:T(8,128)} %copy.11.spring_ref, ...), custom_call_target="tpu_custom_call" | custom-call | tf_op jit(solution)/shard_map/pallas_call | solution.py:595
  71.4 2.1 %copy.16 = bf16[3072,128]{1,0:T(8,128)(2,1)} copy(bf16[3072,128]{1,0:T(8,128)(2,1)} %shard_map.91) | data formatting | bytes 1572864
Async XLA Ops:
  1.9 0.7 copy-start
  2.6 0.7 copy-start.1
